TPU v7x, 32 devices: a whole 2x2x4 slice. The times are simulated.
32 devices in a mesh: groups: 2 (over x), expert: 16 (over z, y, core).
Axes of the slice: x: 2, y: 2, z: 4, core: 2. Of those that a mesh axis runs over, the one named last changes fastest.
Arguments:
- residual: bfloat16 [512, 2880], P(('groups', 'expert')), parts along dimension 0, may hold values from -6 to 6
- norm_gain: float32 [2880], replicated, may hold values from 0.1 to 1.9
- expert_ids: int32 [512, 4], P(('groups', 'expert')), parts along dimension 0, may hold values from 0 to 7, all different within a row; in each aligned block of 16 rows (0 to 15, 16 to 31, ...) at most 16 rows name the same one
- expert_weights: float32 [512, 4], P(('groups', 'expert')), parts along dimension 0, may hold values from 0.2 to 1
- gate_proj: bfloat16 [16, 2880, 720], P('expert'), may hold values from -0.109375 to 0.109375
- up_proj: bfloat16 [16, 2880, 720], P('expert'), may hold values from -0.109375 to 0.109375
- down_proj: bfloat16 [16, 720, 2880], P('expert'), may hold values from -0.15625 to 0.15625
Outputs:
- mixed: bfloat16 [512, 2880], P(('groups', 'expert')), parts along dimension 0
There are 2 independent parts, one for each index of `groups`. A program takes and returns all parts, laid end to end along the dimension named above; an argument that names none is the same for every part. Nothing has to cross between parts.
Inputs may be any that keep to these rules, and one draw needn't show every extreme that they name: `expert_ids`: in each aligned block of 16 rows (the rows of one device) no expert is named by more than 16 entries.
All inputs are finite; a program needn't handle non-finite values.
Results may differ from a plain program's by a relative error of at most 0.0063.
Values may be sent and summed in bfloat16 or wider, within the bound.
A program may use at most 64 MiB of HBM per device.

v0:
```python
import jax
import jax.numpy as jnp
from jax import lax
from jax.sharding import PartitionSpec as P


def partner(value, axis, bit):
    mask = 2**bit
    pairs = [(source, source ^ mask) for source in range(lax.axis_size(axis))]
    return lax.ppermute(value, axis, pairs)


def expert_half(block, gate_w, up_w, down_w):
    flat = block.reshape(-1, block.shape[-1])
    gate = jnp.dot(flat, gate_w, preferred_element_type=jnp.float32)
    upper = jnp.dot(flat, up_w, preferred_element_type=jnp.float32)
    act = (gate * jax.nn.sigmoid(1.702 * gate) * (upper + 1.0)).astype(jnp.bfloat16)
    out = jnp.dot(act, down_w, preferred_element_type=jnp.float32).astype(jnp.bfloat16)
    return out.reshape(block.shape[:-1] + (down_w.shape[1],))


def body(residual, norm_gain, expert_ids, expert_weights, gate_proj, up_proj, down_proj):
    rows, model = residual.shape
    chosen = expert_ids.shape[1]
    devices = lax.axis_size("expert")
    experts = devices // 2
    capacity = 2 * rows * chosen // experts
    half_cap = capacity // 2
    gate_w, up_w, down_w = (gate_proj[0], up_proj[0], down_proj[0])
    x = residual.astype(jnp.float32)
    scale = lax.rsqrt(jnp.mean(x * x, axis=-1, keepdims=True) + 1e-05)
    normed = (x * scale * norm_gain).astype(jnp.bfloat16)
    flat_ids = expert_ids.reshape(rows * chosen)
    onehot = (
        flat_ids[:, None] == lax.broadcasted_iota(jnp.int32, (rows * chosen, experts), 1)
    ).astype(jnp.int32)
    slot = jnp.sum(onehot * jnp.cumsum(onehot, axis=0), axis=1) - 1
    position = flat_ids * capacity + slot
    pick = (
        position[:, None] == lax.broadcasted_iota(jnp.int32, (rows * chosen, experts * capacity), 1)
    ).astype(jnp.float32)
    place_rows = jnp.sum(pick.reshape(rows, chosen, experts * capacity), axis=1)
    send = lax.dot_general(
        place_rows.astype(jnp.bfloat16),
        normed,
        (((0,), (0,)), ((), ())),
        preferred_element_type=jnp.float32,
    )
    send = send.astype(jnp.bfloat16).reshape(experts, capacity, model)
    outgoing = send.reshape(experts, 2, half_cap, model).reshape(devices, half_cap, model)
    arrived = lax.all_to_all(outgoing, "expert", split_axis=0, concat_axis=0, tiled=True)
    other = partner(arrived, "expert", 0)
    both = expert_half(jnp.stack((arrived, other)), gate_w, up_w, down_w)
    returned = partner(both[1], "expert", 0)
    finished = (both[0].astype(jnp.float32) + returned.astype(jnp.float32)).astype(jnp.bfloat16)
    back = lax.all_to_all(finished, "expert", split_axis=0, concat_axis=0, tiled=True)
    results = back.reshape(experts, capacity, model)
    weighted = jnp.sum(
        (pick * expert_weights.reshape(rows * chosen)[:, None]).reshape(
            rows, chosen, experts * capacity
        ),
        axis=1,
    )
    combined = jnp.dot(
        weighted,
        results.reshape(experts * capacity, model).astype(jnp.float32),
        precision=lax.Precision.HIGHEST,
    )
    return (x + combined).astype(jnp.bfloat16)


def solution(mesh):
    in_specs = (
        P(("groups", "expert"), None),
        P(),
        P(("groups", "expert"), None),
        P(("groups", "expert"), None),
        P("expert", None, None),
        P("expert", None, None),
        P("expert", None, None),
    )
    out_specs = P(("groups", "expert"), None)
    return jax.shard_map(body, mesh=mesh, in_specs=in_specs, out_specs=out_specs, check_vma=False)
```

profile of v0, /device:TPU:1, one launch (start us, length us, event | category | flops | bytes accessed | tf_op | source)
XLA Modules:
  0.0 77.1 jit_solution(909006792527382461)
XLA Ops:
  0.0 0.8 copy.23
  0.8 0.1 eq.20
  0.8 0.1 fusion.27
  0.9 0.1 reduce_window_sum.11
  1.0 0.2 select_reduce_fusion.1
  1.2 0.1 sub.7
  1.3 0.1 copy.24
  1.4 0.7 multiply_add_fusion
  2.1 1.0 %fusion.21 = f32[16]{0:T(128)S(1)} fusion(bf16[16,2880]{1,0:T(8,128)(2,1)} %param.7), kind=kLoop, calls=%fused_computation.21 | loop fusion | flops 138224 | bytes 92224 | tf_op jit(solution)/shard_map/reduce_sum | solution.py:31
  3.1 0.8 convert_reduce_fusion
  3.9 1.4 %convolution_convert_fusion = bf16[128,2880]{0,1:T(8,128)(2,1)S(1)} fusion(bf16[16,2880]{1,0:T(8,128)(2,1)} %param.7, f32[2880]{0:T(1024)} %param.8, f32[16]{0:T(128)S(1)} %add_rsqrt_fusion, bf16[16,128]{1,0:T(8,128)(2,1)S(1)} %get-tuple-element.5), kind=kOutput, calls=%fused_computation.7 | convolution fusion | flops 12349440 | bytes 845120 | tf_op jit(solution)/shard_map/dot_general | solution.py:43
  5.3 0.4 copy.25
  5.7 0.0 copy-start.1
  5.7 27.4 %all_to_all.10 = bf16[16,8,2880]{2,1,0:T(8,128)(2,1)S(1)} all-to-all(bf16[16,8,2880]{2,1,0:T(8,128)(2,1)S(1)} %bitcast.34), channel_id=1, replica_groups=mesh['groups'=2,'expert'=16] {'expert'}, dimensions={0} | all-to-all | bytes 1474560 | tf_op jit(solution)/shard_map/all_to_all | solution.py:51
  33.1 0.0 collective-permute-start
  33.1 2.2 %collective-permute-done = bf16[16,8,2880]{2,1,0:T(8,128)(2,1)S(1)} collective-permute-done((bf16[16,8,2880]{2,1,0:T(8,128)(2,1)S(1)}, bf16[16,8,2880]{2,1,0:T(8,128)(2,1)S(1)}, u32[]{:S(2)}, u32[]{:S(2)}) %collective-permute-start) | collective-permute-done | bytes 737312 | tf_op jit(solution)/shard_map/ppermute | solution.py:10
  35.3 0.2 pad_maximum_fusion
  35.5 0.0 copy-done.1
  35.5 1.3 %fusion.4 = f32[256,720]{0,1:T(8,128)S(1)} fusion(bf16[256,2880]{1,0:T(8,128)(2,1)S(1)} %bitcast.35, bf16[1,2880,720]{1,2,0:T(8,128)(2,1)S(1)} %copy-done.1), kind=kOutput, calls=%fused_computation.4 | convolution fusion | flops 1061683200 | bytes 6359040 | tf_op jit(solution)/shard_map/dot_general | solution.py:15
  36.8 9.4 %fusion.6 = bf16[256,2880]{0,1:T(8,128)(2,1)} fusion(bf16[1,720,2880]{2,1,0:T(8,128)(2,1)} %param.13, f32[256,720]{0,1:T(8,128)S(1)} %fusion.4, bf16[256,2880]{1,0:T(8,128)(2,1)S(1)} %bitcast.36, bf16[1,2880,720]{1,2,0:T(8,128)(2,1)} %param.12), kind=kOutput, calls=%fused_computation.6 | convolution fusion | flops 2125578240 | bytes 11980800 | tf_op jit(solution)/shard_map/dot_general | solution.py:18
  46.2 1.5 %fusion.31 = (bf16[128,2880]{0,1:T(8,128)(2,1)S(1)}, f32[128,2880]{0,1:T(8,128)S(1)}) fusion(bf16[256,2880]{0,1:T(8,128)(2,1)} %fusion.6), kind=kLoop, calls=%fused_computation.38 | loop fusion | flops 368640 | bytes 3686400 | tf_op jit(solution)/shard_map/slice | solution.py:54
  47.7 1.2 %copy.27 = bf16[128,2880]{1,0:T(8,128)(2,1)} copy(bf16[128,2880]{0,1:T(8,128)(2,1)S(1)} %get-tuple-element.7) | data formatting | bytes 1474560 | tf_op jit(solution)/shard_map/slice | solution.py:54
  48.9 0.1 collective-permute-start.1
  49.0 0.5 copy.26
  49.5 2.0 %collective-permute-done.1 = bf16[16,8,2880]{2,1,0:T(8,128)(2,1)} collective-permute-done((bf16[16,8,2880]{2,1,0:T(8,128)(2,1)}, bf16[16,8,2880]{2,1,0:T(8,128)(2,1)}, u32[]{:S(2)}, u32[]{:S(2)}) %collective-permute-start.1) | collective-permute-done | bytes 737312 | tf_op jit(solution)/shard_map/ppermute | solution.py:10
  51.5 1.3 %fusion.10 = bf16[16,8,2880]{2,1,0:T(8,128)(2,1)S(1)} fusion(f32[128,2880]{1,0:T(8,128)S(1)} %copy.26, bf16[16,8,2880]{2,1,0:T(8,128)(2,1)} %collective-permute-done.1), kind=kLoop, calls=%fused_computation.12 | loop fusion | flops 1105920 | bytes 2949120 | tf_op jit(solution)/shard_map/convert_element_type | solution.py:55
  52.8 0.0 copy-start
  52.8 23.3 %all_to_all.11 = bf16[16,8,2880]{2,1,0:T(8,128)(2,1)S(1)} all-to-all(bf16[16,8,2880]{2,1,0:T(8,128)(2,1)S(1)} %fusion.10), channel_id=1, replica_groups=mesh['groups'=2,'expert'=16] {'expert'}, dimensions={0} | all-to-all | bytes 1474560 | tf_op jit(solution)/shard_map/all_to_all | solution.py:56
  76.1 0.0 copy-done
  76.1 1.1 %fusion.9 = bf16[16,2880]{1,0:T(8,128)(2,1)} fusion(f32[16,128]{1,0:T(8,128)S(1)} %get-tuple-element.6, bf16[16,8,2880]{2,1,0:T(8,128)(2,1)S(1)} %all_to_all.11, bf16[16,2880]{1,0:T(8,128)(2,1)S(1)} %copy-done), kind=kOutput, calls=%fused_computation.9 | convolution fusion | flops 70917120 | bytes 929792 | tf_op jit(solution)/shard_map/dot_general | solution.py:64
  (2 shorter events, 0.0 us)
Async XLA Ops:
  5.7 29.8 %copy-start.1 = (bf16[1,2880,720]{1,2,0:T(8,128)(2,1)S(1)}, bf16[1,2880,720]{1,2,0:T(8,128)(2,1)}, u32[]{:S(2)}) copy-start(bf16[1,2880,720]{1,2,0:T(8,128)(2,1)} %param.11) | copy-start | bytes 12441604
  33.1 2.2 %collective-permute-start = (bf16[16,8,2880]{2,1,0:T(8,128)(2,1)S(1)}, bf16[16,8,2880]{2,1,0:T(8,128)(2,1)S(1)}, u32[]{:S(2)}, u32[]{:S(2)}) collective-permute-start(bf16[16,8,2880]{2,1,0:T(8,128)(2,1)S(1)} %all_to_all.10), channel_id=1, source_target_pairs={{0,1},{1,0},{2,3},{3,2},{4,5},{5,4},{6,7},{7,6},{8,9},{9,8},{10,11... | collective-permute-start | bytes 2211848 | tf_op jit(solution)/shard_map/ppermute | solution.py:10
  48.9 2.6 %collective-permute-start.1 = (bf16[16,8,2880]{2,1,0:T(8,128)(2,1)}, bf16[16,8,2880]{2,1,0:T(8,128)(2,1)}, u32[]{:S(2)}, u32[]{:S(2)}) collective-permute-start(bf16[16,8,2880]{2,1,0:T(8,128)(2,1)} %bitcast.8), channel_id=1, source_target_pairs={{0,1},{1,0},{2,3},{3,2},{4,5},{5,4},{6,7},{7,6},{8,9},{9,8},{10,11... | collective-permute-start | bytes 2211848 | tf_op jit(solution)/shard_map/ppermute | solution.py:10
  52.8 23.3 %copy-start = (bf16[16,2880]{1,0:T(8,128)(2,1)S(1)}, bf16[16,2880]{1,0:T(8,128)(2,1)}, u32[]{:S(2)}) copy-start(bf16[16,2880]{1,0:T(8,128)(2,1)} %param.7) | copy-start | bytes 276484
where the time goes:
time: 77.5 us; the launch traced here: 77.1 us
  blocking collectives  50.7 us (65%)
  matrix products  13.2 us (17%)
  other arithmetic  5.79 us (7%)
  waiting for transfers between devices  4.22 us (5%)
  local copies, waits for them, and re-layouts  3.03 us (4%)
    all_to_all x1, blocking collectives, body(): lax.all_to_all(outgoing, 'expert', split_axis=0, concat_axis=0, tiled=True)  27.4 us
    all_to_all x1, blocking collectives, body(): lax.all_to_all(finished, 'expert', split_axis=0, concat_axis=0, tiled=True)  23.3 us
    dot_general x1, matrix products, expert_half(): jnp.dot(act, down_w, preferred_element_type=jnp.float32)  9.39 us
    ppermute x2, waiting for transfers between devices, partner(): return lax.ppermute(value, axis, pairs)  4.22 us
  transfers between devices with their start and end apart: 2, of which 2 were waited for; matrix products, arithmetic and copies ran while one was open for 1% of the time, Pallas kernels for 0%

commit v1 on v0

--- a/solution.py
+++ b/solution.py
@@ -1,7 +1,44 @@
+import functools
 import jax
 import jax.numpy as jnp
 from jax import lax
 from jax.sharding import PartitionSpec as P
+
+
+def refer_point_on(xx, where_dim, xin):
+    current_block, opened = (xx.shape[:where_dim], xx.shape[where_dim + 1 :])
+    seen_now = xx.reshape(*current_block, xin, -1, *opened)
+    return jnp.moveaxis(seen_now, where_dim, 0)
+
+
+def form_paths(xs, ndim_at):
+    xs = jnp.moveaxis(xs, 0, ndim_at)
+    passed = xs.shape
+    return xs.reshape(
+        *passed[:ndim_at], passed[ndim_at] * passed[ndim_at + 1], *passed[ndim_at + 2 :]
+    )
+
+
+def supply_view_in(here_x, group_axis, message, point):
+    moved = jax.lax.axis_index(group_axis)
+    current_arr = jax.lax.axis_size(group_axis)
+    row_out, everything = (current_arr, moved)
+    mat_out = refer_point_on(here_x, message, row_out)
+    rack = [mat_out[everything]]
+    tick = 1
+    while tick < row_out:
+        b_next = mat_out[(everything + tick) % row_out]
+        after = jax.lax.ppermute(
+            b_next, group_axis, [(dev_i, (dev_i + tick) % row_out) for dev_i in range(row_out)]
+        )
+        rack.append(after)
+        tick += 1
+    u1 = jnp.stack(rack)
+    mat_out = u1[(everything - jnp.arange(row_out)) % row_out]
+    return form_paths(mat_out, point)
+
+
+_point_plane = functools.partial(supply_view_in, group_axis="expert", message=0, point=0)
 
 
 def partner(value, axis, bit):
@@ -48,7 +85,7 @@
     )
     send = send.astype(jnp.bfloat16).reshape(experts, capacity, model)
     outgoing = send.reshape(experts, 2, half_cap, model).reshape(devices, half_cap, model)
-    arrived = lax.all_to_all(outgoing, "expert", split_axis=0, concat_axis=0, tiled=True)
+    arrived = _point_plane(outgoing)
     other = partner(arrived, "expert", 0)
     both = expert_half(jnp.stack((arrived, other)), gate_w, up_w, down_w)
     returned = partner(both[1], "expert", 0)

time: 77.5 us -> 83.3 us (1.075)
  blocking collectives: 50.7 us -> 26 us
  starting transfers between devices: 0.13 us -> 24.3 us
  waiting for transfers between devices: 4.22 us -> 7.2 us
  matrix products: 13.2 us -> 15.4 us
  local copies, waits for them, and re-layouts: 3.03 us -> 3.95 us
    all_to_all x1 -> x0, blocking collectives: 27.4 us -> none  [body(): lax.all_to_all(outgoing, 'expert', split_axis=0, concat_axis=0, tiled=True)]
    ppermute x0 -> x15, starting transfers between devices: none -> 23.7 us  [supply_view_in(): jax.lax.ppermute(b_next, group_axis, [(dev_i, (dev_i + tick) % row_out) f...]
    ppermute x0 -> x15, waiting for transfers between devices: none -> 3.42 us  [supply_view_in(): jax.lax.ppermute(b_next, group_axis, [(dev_i, (dev_i + tick) % row_out) f...]
    all_to_all x1, blocking collectives: 23.3 us -> 26 us  [body(): lax.all_to_all(finished, 'expert', split_axis=0, concat_axis=0, tiled=True)]
    dot_general x1, matrix products: 1.35 us -> 3.54 us  [expert_half(): gate = jnp.dot(flat, gate_w, preferred_element_type=jnp.float32)]
  transfers between devices with their start and end apart: 2 -> 17, of which waited for: 2 -> 5; matrix products, arithmetic and copies ran while one was open for 1% -> 1% of each run, Pallas kernels for 0% -> 0%
where the time goes in v1:
time: 83.3 us; the launch traced here: 82.9 us
  blocking collectives  26 us (31%)
  starting transfers between devices  24.3 us (29%)
  matrix products  15.4 us (18%)
  waiting for transfers between devices  7.2 us (9%)
  other arithmetic  5.82 us (7%)
  local copies, waits for them, and re-layouts  3.95 us (5%)
    all_to_all x1, blocking collectives, body(): lax.all_to_all(finished, 'expert', split_axis=0, concat_axis=0, tiled=True)  26 us
    ppermute x15, starting transfers between devices, supply_view_in(): jax.lax.ppermute(b_next, group_axis, [(dev_i, (dev_i + tick) % row_out) f...  23.7 us
    dot_general x1, matrix products, expert_half(): jnp.dot(act, down_w, preferred_element_type=jnp.float32)  9.39 us
    ppermute x2, waiting for transfers between devices, partner(): return lax.ppermute(value, axis, pairs)  3.78 us
    dot_general x1, matrix products, expert_half(): gate = jnp.dot(flat, gate_w, preferred_element_type=jnp.float32)  3.54 us
    ppermute x15, waiting for transfers between devices, supply_view_in(): jax.lax.ppermute(b_next, group_axis, [(dev_i, (dev_i + tick) % row_out) f...  3.42 us
  transfers between devices with their start and end apart: 17, of which 5 were waited for; matrix products, arithmetic and copies ran while one was open for 1% of the time, Pallas kernels for 0%

profile of v1, /device:TPU:1, one launch (start us, length us, event | category | flops | bytes accessed | tf_op | source)
XLA Modules:
  0.0 82.9 jit_solution(3718634497645402264)
XLA Ops:
  0.0 0.8 copy.53
  1.4 0.7 multiply_add_fusion
  2.1 1.0 %fusion.21 = f32[16]{0:T(128)S(1)} fusion(bf16[16,2880]{1,0:T(8,128)(2,1)} %param.7), kind=kLoop, calls=%fused_computation.22 | loop fusion | flops 138224 | bytes 92224 | tf_op jit(solution)/shard_map/reduce_sum | solution.py:68
  3.1 0.8 convert_reduce_fusion
  3.9 1.4 %convolution_convert_fusion = bf16[128,2880]{0,1:T(8,128)(2,1)S(1)} fusion(bf16[16,2880]{1,0:T(8,128)(2,1)} %param.7, f32[2880]{0:T(1024)} %param.8, f32[16]{0:T(128)S(1)} %add_rsqrt_fusion, bf16[16,128]{1,0:T(8,128)(2,1)S(1)} %get-tuple-element.5), kind=kOutput, calls=%fused_computation.8 | convolution fusion | flops 12349440 | bytes 845120 | tf_op jit(solution)/shard_map/dot_general | solution.py:80
  5.3 0.4 copy.55
  5.9 2.7 %collective-permute-start = (bf16[1,8,2880]{2,1,0:T(8,128)(2,1)S(1)}, bf16[1,8,2880]{2,1,0:T(8,128)(2,1)S(1)}, u32[]{:S(2)}, u32[]{:S(2)}) collective-permute-start(bf16[1,8,2880]{2,1,0:T(8,128)(2,1)S(1)} %get-tuple-element.23), channel_id=1, source_target_pairs={{0,1},{1,2},{2,3},{3,4},{4,5},{5,6},{6,7},{7,8},{8,9},{9,10},{10,1... | collective-permute-start | bytes 138248 | tf_op jit(solution)/shard_map/ppermute | solution.py:31
  8.5 1.2 %collective-permute-start.1 = (bf16[1,8,2880]{2,1,0:T(8,128)(2,1)S(1)}, bf16[1,8,2880]{2,1,0:T(8,128)(2,1)S(1)}, u32[]{:S(2)}, u32[]{:S(2)}) collective-permute-start(bf16[1,8,2880]{2,1,0:T(8,128)(2,1)S(1)} %get-tuple-element.22), channel_id=1, source_target_pairs={{0,2},{1,3},{2,4},{3,5},{4,6},{5,7},{6,8},{7,9},{8,10},{9,11},{10,... | collective-permute-start | bytes 138248 | tf_op jit(solution)/shard_map/ppermute | solution.py:31
  9.8 0.4 collective-permute-start.2
  10.2 1.3 %collective-permute-start.3 = (bf16[1,8,2880]{2,1,0:T(8,128)(2,1)S(1)}, bf16[1,8,2880]{2,1,0:T(8,128)(2,1)S(1)}, u32[]{:S(2)}, u32[]{:S(2)}) collective-permute-start(bf16[1,8,2880]{2,1,0:T(8,128)(2,1)S(1)} %get-tuple-element.20), channel_id=1, source_target_pairs={{0,4},{1,5},{2,6},{3,7},{4,8},{5,9},{6,10},{7,11},{8,12},{9,13},{1... | collective-permute-start | bytes 138248 | tf_op jit(solution)/shard_map/ppermute | solution.py:31
  11.5 2.4 %collective-permute-start.4 = (bf16[1,8,2880]{2,1,0:T(8,128)(2,1)S(1)}, bf16[1,8,2880]{2,1,0:T(8,128)(2,1)S(1)}, u32[]{:S(2)}, u32[]{:S(2)}) collective-permute-start(bf16[1,8,2880]{2,1,0:T(8,128)(2,1)S(1)} %get-tuple-element.19), channel_id=1, source_target_pairs={{0,5},{1,6},{2,7},{3,8},{4,9},{5,10},{6,11},{7,12},{8,13},{9,14},{... | collective-permute-start | bytes 138248 | tf_op jit(solution)/shard_map/ppermute | solution.py:31
  13.9 2.2 %collective-permute-start.5 = (bf16[1,8,2880]{2,1,0:T(8,128)(2,1)S(1)}, bf16[1,8,2880]{2,1,0:T(8,128)(2,1)S(1)}, u32[]{:S(2)}, u32[]{:S(2)}) collective-permute-start(bf16[1,8,2880]{2,1,0:T(8,128)(2,1)S(1)} %get-tuple-element.18), channel_id=1, source_target_pairs={{0,6},{1,7},{2,8},{3,9},{4,10},{5,11},{6,12},{7,13},{8,14},{9,15},... | collective-permute-start | bytes 138248 | tf_op jit(solution)/shard_map/ppermute | solution.py:31
  16.1 0.6 collective-permute-start.6
  16.7 1.0 %collective-permute-start.7 = (bf16[1,8,2880]{2,1,0:T(8,128)(2,1)S(1)}, bf16[1,8,2880]{2,1,0:T(8,128)(2,1)S(1)}, u32[]{:S(2)}, u32[]{:S(2)}) collective-permute-start(bf16[1,8,2880]{2,1,0:T(8,128)(2,1)S(1)} %get-tuple-element.16), channel_id=1, source_target_pairs={{0,8},{1,9},{2,10},{3,11},{4,12},{5,13},{6,14},{7,15},{8,0},{9,1},... | collective-permute-start | bytes 138248 | tf_op jit(solution)/shard_map/ppermute | solution.py:31
  17.7 3.8 %collective-permute-start.8 = (bf16[1,8,2880]{2,1,0:T(8,128)(2,1)S(1)}, bf16[1,8,2880]{2,1,0:T(8,128)(2,1)S(1)}, u32[]{:S(2)}, u32[]{:S(2)}) collective-permute-start(bf16[1,8,2880]{2,1,0:T(8,128)(2,1)S(1)} %get-tuple-element.15), channel_id=1, source_target_pairs={{0,9},{1,10},{2,11},{3,12},{4,13},{5,14},{6,15},{7,0},{8,1},{9,2},... | collective-permute-start | bytes 138248 | tf_op jit(solution)/shard_map/ppermute | solution.py:31
  21.6 2.0 %collective-permute-start.9 = (bf16[1,8,2880]{2,1,0:T(8,128)(2,1)S(1)}, bf16[1,8,2880]{2,1,0:T(8,128)(2,1)S(1)}, u32[]{:S(2)}, u32[]{:S(2)}) collective-permute-start(bf16[1,8,2880]{2,1,0:T(8,128)(2,1)S(1)} %get-tuple-element.14), channel_id=1, source_target_pairs={{0,10},{1,11},{2,12},{3,13},{4,14},{5,15},{6,0},{7,1},{8,2},{9,3},... | collective-permute-start | bytes 138248 | tf_op jit(solution)/shard_map/ppermute | solution.py:31
  23.7 0.7 collective-permute-start.11
  24.5 3.6 %collective-permute-start.12 = (bf16[1,8,2880]{2,1,0:T(8,128)(2,1)S(1)}, bf16[1,8,2880]{2,1,0:T(8,128)(2,1)S(1)}, u32[]{:S(2)}, u32[]{:S(2)}) collective-permute-start(bf16[1,8,2880]{2,1,0:T(8,128)(2,1)S(1)} %get-tuple-element.11), channel_id=1, source_target_pairs={{0,13},{1,14},{2,15},{3,0},{4,1},{5,2},{6,3},{7,4},{8,5},{9,6},{10... | collective-permute-start | bytes 138248 | tf_op jit(solution)/shard_map/ppermute | solution.py:31
  28.1 1.6 %collective-permute-start.13 = (bf16[1,8,2880]{2,1,0:T(8,128)(2,1)S(1)}, bf16[1,8,2880]{2,1,0:T(8,128)(2,1)S(1)}, u32[]{:S(2)}, u32[]{:S(2)}) collective-permute-start(bf16[1,8,2880]{2,1,0:T(8,128)(2,1)S(1)} %get-tuple-element.10), channel_id=1, source_target_pairs={{0,14},{1,15},{2,0},{3,1},{4,2},{5,3},{6,4},{7,5},{8,6},{9,7},{10,... | collective-permute-start | bytes 138248 | tf_op jit(solution)/shard_map/ppermute | solution.py:31
  29.9 1.2 %collective-permute-done.13 = bf16[1,8,2880]{2,1,0:T(8,128)(2,1)S(1)} collective-permute-done((bf16[1,8,2880]{2,1,0:T(8,128)(2,1)S(1)}, bf16[1,8,2880]{2,1,0:T(8,128)(2,1)S(1)}, u32[]{:S(2)}, u32[]{:S(2)}) %collective-permute-start.13) | collective-permute-done | bytes 46112 | tf_op jit(solution)/shard_map/ppermute | solution.py:31
  31.1 2.2 %collective-permute-done.14 = bf16[1,8,2880]{2,1,0:T(8,128)(2,1)S(1)} collective-permute-done((bf16[1,8,2880]{2,1,0:T(8,128)(2,1)S(1)}, bf16[1,8,2880]{2,1,0:T(8,128)(2,1)S(1)}, u32[]{:S(2)}, u32[]{:S(2)}) %collective-permute-start.14) | collective-permute-done | bytes 46112 | tf_op jit(solution)/shard_map/ppermute | solution.py:31
  33.2 0.6 gather_fusion
  34.2 2.0 %collective-permute-done.15 = bf16[16,8,2880]{2,1,0:T(8,128)(2,1)S(1)} collective-permute-done((bf16[16,8,2880]{2,1,0:T(8,128)(2,1)S(1)}, bf16[16,8,2880]{2,1,0:T(8,128)(2,1)S(1)}, u32[]{:S(2)}, u32[]{:S(2)}) %collective-permute-start.15) | collective-permute-done | bytes 737312 | tf_op jit(solution)/shard_map/ppermute | solution.py:47
  36.3 3.5 %fusion.4 = f32[256,720]{0,1:T(8,128)S(1)} fusion(bf16[256,2880]{1,0:T(8,128)(2,1)S(1)} %bitcast.128, bf16[1,2880,720]{1,2,0:T(8,128)(2,1)} %param.11), kind=kOutput, calls=%fused_computation.5 | convolution fusion | flops 1061683200 | bytes 6359040 | tf_op jit(solution)/shard_map/dot_general | solution.py:52
  39.9 9.4 %fusion.6 = bf16[256,2880]{0,1:T(8,128)(2,1)} fusion(bf16[1,720,2880]{2,1,0:T(8,128)(2,1)} %param.13, f32[256,720]{0,1:T(8,128)S(1)} %fusion.4, bf16[256,2880]{1,0:T(8,128)(2,1)S(1)} %bitcast.129, bf16[1,2880,720]{1,2,0:T(8,128)(2,1)} %param.12), kind=kOutput, calls=%fused_computation.7 | convolution fusion | flops 2125578240 | bytes 11980800 | tf_op jit(solution)/shard_map/dot_general | solution.py:55
  49.3 1.5 %fusion.33 = (bf16[128,2880]{0,1:T(8,128)(2,1)S(1)}, f32[128,2880]{0,1:T(8,128)S(1)}) fusion(bf16[256,2880]{0,1:T(8,128)(2,1)} %fusion.6), kind=kLoop, calls=%fused_computation.77 | loop fusion | flops 368640 | bytes 3686400 | tf_op jit(solution)/shard_map/slice | solution.py:91
  50.8 1.2 %copy.72 = bf16[128,2880]{1,0:T(8,128)(2,1)} copy(bf16[128,2880]{0,1:T(8,128)(2,1)S(1)} %get-tuple-element.7) | data formatting | bytes 1474560 | tf_op jit(solution)/shard_map/slice | solution.py:91
  52.2 0.5 copy.71
  52.7 1.8 %collective-permute-done.16 = bf16[16,8,2880]{2,1,0:T(8,128)(2,1)} collective-permute-done((bf16[16,8,2880]{2,1,0:T(8,128)(2,1)}, bf16[16,8,2880]{2,1,0:T(8,128)(2,1)}, u32[]{:S(2)}, u32[]{:S(2)}) %collective-permute-start.16) | collective-permute-done | bytes 737312 | tf_op jit(solution)/shard_map/ppermute | solution.py:47
  54.5 1.3 %fusion.10 = bf16[16,8,2880]{2,1,0:T(8,128)(2,1)S(1)} fusion(f32[128,2880]{1,0:T(8,128)S(1)} %copy.71, bf16[16,8,2880]{2,1,0:T(8,128)(2,1)} %collective-permute-done.16), kind=kLoop, calls=%fused_computation.13 | loop fusion | flops 1105920 | bytes 2949120 | tf_op jit(solution)/shard_map/convert_element_type | solution.py:92
  55.8 26.0 %all_to_all.5 = bf16[16,8,2880]{2,1,0:T(8,128)(2,1)S(1)} all-to-all(bf16[16,8,2880]{2,1,0:T(8,128)(2,1)S(1)} %fusion.10), channel_id=1, replica_groups=mesh['groups'=2,'expert'=16] {'expert'}, dimensions={0} | all-to-all | bytes 1474560 | tf_op jit(solution)/shard_map/all_to_all | solution.py:93
  81.8 1.1 %fusion.9 = bf16[16,2880]{1,0:T(8,128)(2,1)} fusion(f32[16,128]{1,0:T(8,128)S(1)} %get-tuple-element.6, bf16[16,8,2880]{2,1,0:T(8,128)(2,1)S(1)} %all_to_all.5, bf16[16,2880]{1,0:T(8,128)(2,1)S(1)} %copy-done), kind=kOutput, calls=%fused_computation.10 | convolution fusion | flops 70917120 | bytes 929792 | tf_op jit(solution)/shard_map/dot_general | solution.py:101
  (46 shorter events, 2.1 us)
Async XLA Ops:
  5.9 8.1 %collective-permute-start = (bf16[1,8,2880]{2,1,0:T(8,128)(2,1)S(1)}, bf16[1,8,2880]{2,1,0:T(8,128)(2,1)S(1)}, u32[]{:S(2)}, u32[]{:S(2)}) collective-permute-start(bf16[1,8,2880]{2,1,0:T(8,128)(2,1)S(1)} %get-tuple-element.23), channel_id=1, source_target_pairs={{0,1},{1,2},{2,3},{3,4},{4,5},{5,6},{6,7},{7,8},{8,9},{9,10},{10,1... | collective-permute-start | bytes 138248 | tf_op jit(solution)/shard_map/ppermute | solution.py:31
  8.5 7.6 %collective-permute-start.1 = (bf16[1,8,2880]{2,1,0:T(8,128)(2,1)S(1)}, bf16[1,8,2880]{2,1,0:T(8,128)(2,1)S(1)}, u32[]{:S(2)}, u32[]{:S(2)}) collective-permute-start(bf16[1,8,2880]{2,1,0:T(8,128)(2,1)S(1)} %get-tuple-element.22), channel_id=1, source_target_pairs={{0,2},{1,3},{2,4},{3,5},{4,6},{5,7},{6,8},{7,9},{8,10},{9,11},{10,... | collective-permute-start | bytes 138248 | tf_op jit(solution)/shard_map/ppermute | solution.py:31
  9.8 6.9 %collective-permute-start.2 = (bf16[1,8,2880]{2,1,0:T(8,128)(2,1)S(1)}, bf16[1,8,2880]{2,1,0:T(8,128)(2,1)S(1)}, u32[]{:S(2)}, u32[]{:S(2)}) collective-permute-start(bf16[1,8,2880]{2,1,0:T(8,128)(2,1)S(1)} %get-tuple-element.21), channel_id=1, source_target_pairs={{0,3},{1,4},{2,5},{3,6},{4,7},{5,8},{6,9},{7,10},{8,11},{9,12},{10... | collective-permute-start | bytes 138248 | tf_op jit(solution)/shard_map/ppermute | solution.py:31
  10.2 7.5 %collective-permute-start.3 = (bf16[1,8,2880]{2,1,0:T(8,128)(2,1)S(1)}, bf16[1,8,2880]{2,1,0:T(8,128)(2,1)S(1)}, u32[]{:S(2)}, u32[]{:S(2)}) collective-permute-start(bf16[1,8,2880]{2,1,0:T(8,128)(2,1)S(1)} %get-tuple-element.20), channel_id=1, source_target_pairs={{0,4},{1,5},{2,6},{3,7},{4,8},{5,9},{6,10},{7,11},{8,12},{9,13},{1... | collective-permute-start | bytes 138248 | tf_op jit(solution)/shard_map/ppermute | solution.py:31
  11.5 10.1 %collective-permute-start.4 = (bf16[1,8,2880]{2,1,0:T(8,128)(2,1)S(1)}, bf16[1,8,2880]{2,1,0:T(8,128)(2,1)S(1)}, u32[]{:S(2)}, u32[]{:S(2)}) collective-permute-start(bf16[1,8,2880]{2,1,0:T(8,128)(2,1)S(1)} %get-tuple-element.19), channel_id=1, source_target_pairs={{0,5},{1,6},{2,7},{3,8},{4,9},{5,10},{6,11},{7,12},{8,13},{9,14},{... | collective-permute-start | bytes 138248 | tf_op jit(solution)/shard_map/ppermute | solution.py:31
  13.9 9.6 %collective-permute-start.5 = (bf16[1,8,2880]{2,1,0:T(8,128)(2,1)S(1)}, bf16[1,8,2880]{2,1,0:T(8,128)(2,1)S(1)}, u32[]{:S(2)}, u32[]{:S(2)}) collective-permute-start(bf16[1,8,2880]{2,1,0:T(8,128)(2,1)S(1)} %get-tuple-element.18), channel_id=1, source_target_pairs={{0,6},{1,7},{2,8},{3,9},{4,10},{5,11},{6,12},{7,13},{8,14},{9,15},... | collective-permute-start | bytes 138248 | tf_op jit(solution)/shard_map/ppermute | solution.py:31
  16.1 7.6 %collective-permute-start.6 = (bf16[1,8,2880]{2,1,0:T(8,128)(2,1)S(1)}, bf16[1,8,2880]{2,1,0:T(8,128)(2,1)S(1)}, u32[]{:S(2)}, u32[]{:S(2)}) collective-permute-start(bf16[1,8,2880]{2,1,0:T(8,128)(2,1)S(1)} %get-tuple-element.17), channel_id=1, source_target_pairs={{0,7},{1,8},{2,9},{3,10},{4,11},{5,12},{6,13},{7,14},{8,15},{9,0},... | collective-permute-start | bytes 138248 | tf_op jit(solution)/shard_map/ppermute | solution.py:31
  16.7 7.7 %collective-permute-start.7 = (bf16[1,8,2880]{2,1,0:T(8,128)(2,1)S(1)}, bf16[1,8,2880]{2,1,0:T(8,128)(2,1)S(1)}, u32[]{:S(2)}, u32[]{:S(2)}) collective-permute-start(bf16[1,8,2880]{2,1,0:T(8,128)(2,1)S(1)} %get-tuple-element.16), channel_id=1, source_target_pairs={{0,8},{1,9},{2,10},{3,11},{4,12},{5,13},{6,14},{7,15},{8,0},{9,1},... | collective-permute-start | bytes 138248 | tf_op jit(solution)/shard_map/ppermute | solution.py:31
  17.7 10.4 %collective-permute-start.8 = (bf16[1,8,2880]{2,1,0:T(8,128)(2,1)S(1)}, bf16[1,8,2880]{2,1,0:T(8,128)(2,1)S(1)}, u32[]{:S(2)}, u32[]{:S(2)}) collective-permute-start(bf16[1,8,2880]{2,1,0:T(8,128)(2,1)S(1)} %get-tuple-element.15), channel_id=1, source_target_pairs={{0,9},{1,10},{2,11},{3,12},{4,13},{5,14},{6,15},{7,0},{8,1},{9,2},... | collective-permute-start | bytes 138248 | tf_op jit(solution)/shard_map/ppermute | solution.py:31
  21.6 8.1 %collective-permute-start.9 = (bf16[1,8,2880]{2,1,0:T(8,128)(2,1)S(1)}, bf16[1,8,2880]{2,1,0:T(8,128)(2,1)S(1)}, u32[]{:S(2)}, u32[]{:S(2)}) collective-permute-start(bf16[1,8,2880]{2,1,0:T(8,128)(2,1)S(1)} %get-tuple-element.14), channel_id=1, source_target_pairs={{0,10},{1,11},{2,12},{3,13},{4,14},{5,15},{6,0},{7,1},{8,2},{9,3},... | collective-permute-start | bytes 138248 | tf_op jit(solution)/shard_map/ppermute | solution.py:31
  23.5 6.2 %collective-permute-start.10 = (bf16[1,8,2880]{2,1,0:T(8,128)(2,1)S(1)}, bf16[1,8,2880]{2,1,0:T(8,128)(2,1)S(1)}, u32[]{:S(2)}, u32[]{:S(2)}) collective-permute-start(bf16[1,8,2880]{2,1,0:T(8,128)(2,1)S(1)} %get-tuple-element.13), channel_id=1, source_target_pairs={{0,11},{1,12},{2,13},{3,14},{4,15},{5,0},{6,1},{7,2},{8,3},{9,4},{... | collective-permute-start | bytes 138248 | tf_op jit(solution)/shard_map/ppermute | solution.py:31
  23.7 6.0 %collective-permute-start.11 = (bf16[1,8,2880]{2,1,0:T(8,128)(2,1)S(1)}, bf16[1,8,2880]{2,1,0:T(8,128)(2,1)S(1)}, u32[]{:S(2)}, u32[]{:S(2)}) collective-permute-start(bf16[1,8,2880]{2,1,0:T(8,128)(2,1)S(1)} %get-tuple-element.12), channel_id=1, source_target_pairs={{0,12},{1,13},{2,14},{3,15},{4,0},{5,1},{6,2},{7,3},{8,4},{9,5},{1... | collective-permute-start | bytes 138248 | tf_op jit(solution)/shard_map/ppermute | solution.py:31
  24.5 5.4 %collective-permute-start.12 = (bf16[1,8,2880]{2,1,0:T(8,128)(2,1)S(1)}, bf16[1,8,2880]{2,1,0:T(8,128)(2,1)S(1)}, u32[]{:S(2)}, u32[]{:S(2)}) collective-permute-start(bf16[1,8,2880]{2,1,0:T(8,128)(2,1)S(1)} %get-tuple-element.11), channel_id=1, source_target_pairs={{0,13},{1,14},{2,15},{3,0},{4,1},{5,2},{6,3},{7,4},{8,5},{9,6},{10... | collective-permute-start | bytes 138248 | tf_op jit(solution)/shard_map/ppermute | solution.py:31
  28.1 3.0 %collective-permute-start.13 = (bf16[1,8,2880]{2,1,0:T(8,128)(2,1)S(1)}, bf16[1,8,2880]{2,1,0:T(8,128)(2,1)S(1)}, u32[]{:S(2)}, u32[]{:S(2)}) collective-permute-start(bf16[1,8,2880]{2,1,0:T(8,128)(2,1)S(1)} %get-tuple-element.10), channel_id=1, source_target_pairs={{0,14},{1,15},{2,0},{3,1},{4,2},{5,3},{6,4},{7,5},{8,6},{9,7},{10,... | collective-permute-start | bytes 138248 | tf_op jit(solution)/shard_map/ppermute | solution.py:31
  29.7 3.5 %collective-permute-start.14 = (bf16[1,8,2880]{2,1,0:T(8,128)(2,1)S(1)}, bf16[1,8,2880]{2,1,0:T(8,128)(2,1)S(1)}, u32[]{:S(2)}, u32[]{:S(2)}) collective-permute-start(bf16[1,8,2880]{2,1,0:T(8,128)(2,1)S(1)} %get-tuple-element.9), channel_id=1, source_target_pairs={{0,15},{1,0},{2,1},{3,2},{4,3},{5,4},{6,5},{7,6},{8,7},{9,8},{10,9... | collective-permute-start | bytes 138248 | tf_op jit(solution)/shard_map/ppermute | solution.py:31
  33.9 2.3 %collective-permute-start.15 = (bf16[16,8,2880]{2,1,0:T(8,128)(2,1)S(1)}, bf16[16,8,2880]{2,1,0:T(8,128)(2,1)S(1)}, u32[]{:S(2)}, u32[]{:S(2)}) collective-permute-start(bf16[16,8,2880]{2,1,0:T(8,128)(2,1)S(1)} %gather_fusion), channel_id=1, source_target_pairs={{0,1},{1,0},{2,3},{3,2},{4,5},{5,4},{6,7},{7,6},{8,9},{9,8},{10,11... | collective-permute-start | bytes 2211848 | tf_op jit(solution)/shard_map/ppermute | solution.py:47
  51.9 2.6 %collective-permute-start.16 = (bf16[16,8,2880]{2,1,0:T(8,128)(2,1)}, bf16[16,8,2880]{2,1,0:T(8,128)(2,1)}, u32[]{:S(2)}, u32[]{:S(2)}) collective-permute-start(bf16[16,8,2880]{2,1,0:T(8,128)(2,1)} %bitcast.55), channel_id=1, source_target_pairs={{0,1},{1,0},{2,3},{3,2},{4,5},{5,4},{6,7},{7,6},{8,9},{9,8},{10,11... | collective-permute-start | bytes 2211848 | tf_op jit(solution)/shard_map/ppermute | solution.py:47
  55.8 26.0 %copy-start = (bf16[16,2880]{1,0:T(8,128)(2,1)S(1)}, bf16[16,2880]{1,0:T(8,128)(2,1)}, u32[]{:S(2)}) copy-start(bf16[16,2880]{1,0:T(8,128)(2,1)} %param.7) | copy-start | bytes 276484
